TPU v7x, 256 devices: a whole 4x4x8 slice. The times are simulated.
256 devices in a mesh: rep: 32 (over y, z), shard: 8 (over x, core).
Axes of the slice: x: 4, y: 4, z: 8, core: 2. Of those that a mesh axis runs over, the one named last changes fastest.
Arguments:
- gradient: bfloat16 [32, 1024, 4096], P('rep', None, 'shard'), may hold values from -16 to 16
- feedback: bfloat16 [32, 1024, 4096], P('rep', None, 'shard'), may hold values from -4 to 4
- warm_start: float32 [1024, 64], replicated, may hold values from -6 to 6
- master: float32 [1024, 4096], P('rep', 'shard'), may hold values from -4 to 4
- moment: float32 [1024, 4096], P('rep', 'shard'), may hold values from -1.5 to 1.5
- second: float32 [1024, 4096], P('rep', 'shard'), may hold values from 0.005 to 0.5
Outputs:
- new_feedback: bfloat16 [32, 1024, 4096], P('rep', None, 'shard')
- weights: bfloat16 [1024, 4096], P(None, 'shard')
- master_out: float32 [1024, 4096], P('rep', 'shard')
- moment_out: float32 [1024, 4096], P('rep', 'shard')
- second_out: float32 [1024, 4096], P('rep', 'shard')
- right_factor: float32 [1024, 64], replicated
All inputs are finite; a program needn't handle non-finite values.
Results may differ from a plain program's by a relative error of at most 0.001.
Values may be sent and summed in bfloat16 or wider, within the bound.
No kernel may reach another device: no remote copies, remote signals or barrier semaphores. Data moves between devices by JAX's collectives and lax.ppermute only.
A program may use at most 64 MiB of HBM per device.

v0:
```python
import jax
import jax.numpy as jnp
from jax import lax
from jax.sharding import PartitionSpec as P

HIGHEST = lax.Precision.HIGHEST
beta_one = 0.9
beta_two = 0.95
learn_rate = 0.02
decay_rate = 0.1
adam_eps = 1e-08
ridge_rate = 1e-06


def lower_inverse(gram):
    matrix_order = gram.shape[0]
    identity = jnp.eye(matrix_order, dtype=jnp.float32)
    ridge_term = ridge_rate * jnp.trace(gram) / matrix_order
    cholesky_lower = jnp.linalg.cholesky(gram + ridge_term * identity)
    return jax.scipy.linalg.solve_triangular(cholesky_lower, identity, lower=True)


def contract_first(left, right):
    return lax.dot_general(
        left, right, (((0,), (0,)), ((), ())), precision=HIGHEST, preferred_element_type=jnp.float32
    )


def times_inverse(left, inverse):
    return jnp.dot(left, inverse.T, precision=HIGHEST, preferred_element_type=jnp.float32)


def on_device(gradient, feedback, warm_start, master, moment, second):
    replicas = lax.axis_size("rep")
    merged = gradient[0].astype(jnp.float32) + feedback[0].astype(jnp.float32)
    local_factor = contract_first(merged, warm_start)
    factor = lax.psum(local_factor, "rep") / replicas
    gram_part = contract_first(factor, factor)
    gram = lax.psum(gram_part, "shard")
    inverse = lower_inverse(gram)
    unit_basis = times_inverse(factor, inverse)
    projected = jnp.dot(merged, unit_basis, precision=HIGHEST, preferred_element_type=jnp.float32)
    right_factor = lax.psum(projected, ("rep", "shard")) / replicas
    approx = lax.dot_general(
        right_factor,
        unit_basis,
        (((1,), (1,)), ((), ())),
        precision=HIGHEST,
        preferred_element_type=jnp.float32,
    )
    new_feedback = (merged - approx).astype(jnp.bfloat16)[None]
    own_rows = master.shape[0]
    row_start = lax.axis_index("rep") * own_rows
    grad_rows = lax.dynamic_slice_in_dim(approx, row_start, own_rows, 0)
    moment_out = beta_one * moment + (1.0 - beta_one) * grad_rows
    second_out = beta_two * second + (1.0 - beta_two) * grad_rows * grad_rows
    master_out = master - learn_rate * (
        moment_out / (jnp.sqrt(second_out) + adam_eps) + decay_rate * master
    )
    weights = lax.all_gather(master_out.astype(jnp.bfloat16), "rep", axis=0, tiled=True)
    return (new_feedback, weights, master_out, moment_out, second_out, right_factor)


def solution(mesh):
    return jax.shard_map(
        on_device,
        mesh=mesh,
        in_specs=(
            P("rep", None, "shard"),
            P("rep", None, "shard"),
            P(),
            P("rep", "shard"),
            P("rep", "shard"),
            P("rep", "shard"),
        ),
        out_specs=(
            P("rep", None, "shard"),
            P(None, "shard"),
            P("rep", "shard"),
            P("rep", "shard"),
            P("rep", "shard"),
            P(),
        ),
        check_vma=False,
    )
```

profile of v0, /device:TPU:2, one launch (start us, length us, event | category | flops | bytes accessed | tf_op | source)
XLA Modules:
  0.0 533.7 jit_solution(15276774667782180067)
XLA Ops:
  7.2 0.0 copy-start
  7.2 0.0 copy-start.1
  7.2 0.0 copy-start.2
  7.2 0.0 all-reduce.3.cloned.1.call-start
  7.2 0.9 copy-done
  8.1 3.8 fusion.2
  12.0 0.0 all-reduce.3.cloned.1.call-update
  12.0 0.0 all-reduce.5.cloned.1.call-start
  12.0 143.7 %all-reduce.3.cloned.1.call-done = f32[512,64]{0,1:T(8,128)} async-done(((f32[512,64]{0,1:T(8,128)}), f32[512,64]{0,1:T(8,128)}) %all-reduce.3.cloned.1.call-update) | async-done | bytes 131088 | tf_op jit(solution)/shard_map/psum | solution.py:37
  155.8 1.2 fusion.8
  157.0 20.7 %psum.22 = f32[64,64]{1,0:T(8,128)S(1)} all-reduce(f32[64,64]{1,0:T(8,128)S(1)} %fusion.8), channel_id=1, replica_groups=mesh['rep'=32,'shard'=8] {'shard'}, use_global_device_ids=true, to_apply=%region_1.0 | all-reduce | flops 4096 | bytes 32768 | tf_op jit(solution)/shard_map/psum | solution.py:39
  177.7 0.6 select_reduce_fusion.1
  179.0 0.1 copy.12
  179.1 5.8 %cholesky.18 = f32[64,64]{1,0:T(8,128)S(1)} custom-call(f32[64,64]{1,0:T(8,128)S(1)} %fusion.16), custom_call_target="Cholesky" | custom-call | tf_op jit(solution)/shard_map/jit(cholesky)/cholesky | solution.py:19
  185.0 0.6 compare_reduce_fusion
  185.6 0.7 fusion.13
  186.3 4.9 custom-call.7
  191.2 0.2 fusion.14
  191.4 1.2 fusion.6
  192.6 0.0 copy-done.1
  192.6 0.0 copy-done.2
  192.6 3.0 fusion
  195.6 0.0 copy-start.5
  195.6 0.0 copy-start.6
  195.6 0.0 copy-start.7
  195.6 0.0 all-reduce.5.cloned.1.call-update
  195.7 0.0 all-gather.2.cloned.1.call-start
  195.7 249.2 %all-reduce.5.cloned.1.call-done = f32[1024,64]{0,1:T(8,128)} async-done(((f32[1024,64]{0,1:T(8,128)}), f32[1024,64]{0,1:T(8,128)}) %all-reduce.5.cloned.1.call-update) | async-done | bytes 262160 | tf_op jit(solution)/shard_map/psum | solution.py:43
  444.9 1.0 broadcast_multiply_fusion
  445.9 0.0 copy-start.4
  445.9 1.8 fusion.21
  447.8 0.0 copy-start.3
  447.8 1.3 copy-done.3
  449.1 0.0 copy-done.5
  449.1 0.0 copy-done.6
  449.1 0.0 copy-done.7
  449.1 0.7 fusion.19
  449.8 0.0 all-gather.2.cloned.1.call-update
  449.9 3.0 fusion.5
  452.9 0.0 copy-done.4
  452.9 72.0 %all-gather.2.cloned.1.call-done = bf16[1024,512]{1,0:T(8,128)(2,1)} async-done(((bf16[32,512]{1,0:T(8,128)(2,1)}), bf16[1024,512]{1,0:T(8,128)(2,1)}) %all-gather.2.cloned.1.call-update) | async-done | bytes 1048592 | tf_op jit(solution)/shard_map/all_gather | solution.py:60
  524.9 2.3 copy.16
  (3 shorter events, 0.1 us)
Async XLA Ops:
  7.2 1.0 copy-start
  7.2 185.4 %copy-start.1 = (bf16[1,1024,512]{2,1,0:T(8,128)(2,1)S(1)}, bf16[1,1024,512]{2,1,0:T(8,128)(2,1)}, u32[]{:S(2)}) copy-start(bf16[1,1024,512]{2,1,0:T(8,128)(2,1)} %param.7) | copy-start | bytes 3145732
  7.2 185.4 %copy-start.2 = (bf16[1,1024,512]{2,1,0:T(8,128)(2,1)S(1)}, bf16[1,1024,512]{2,1,0:T(8,128)(2,1)}, u32[]{:S(2)}) copy-start(bf16[1,1024,512]{2,1,0:T(8,128)(2,1)} %param.6) | copy-start | bytes 3145732
  7.2 148.6 %all-reduce.3.cloned.1.call-start = ((), (), s32[]{:S(2)}) async-start(), calls=%async_computation | async-start | bytes 262144 | tf_op jit(solution)/shard_map/psum | solution.py:37
  12.0 432.9 %all-reduce.5.cloned.1.call-start = ((), (), s32[]{:S(2)}) async-start(), calls=%async_computation.1 | async-start | bytes 524288 | tf_op jit(solution)/shard_map/psum | solution.py:43
  195.6 253.5 %copy-start.5 = (f32[32,512]{1,0:T(8,128)S(1)}, f32[32,512]{1,0:T(8,128)}, u32[]{:S(2)}) copy-start(f32[32,512]{1,0:T(8,128)} %param.9) | copy-start | bytes 196612
  195.6 253.5 %copy-start.6 = (f32[32,512]{1,0:T(8,128)S(1)}, f32[32,512]{1,0:T(8,128)}, u32[]{:S(2)}) copy-start(f32[32,512]{1,0:T(8,128)} %param.11) | copy-start | bytes 196612
  195.6 253.5 %copy-start.7 = (f32[32,512]{1,0:T(8,128)S(1)}, f32[32,512]{1,0:T(8,128)}, u32[]{:S(2)}) copy-start(f32[32,512]{1,0:T(8,128)} %param.10) | copy-start | bytes 196612
  195.7 329.2 %all-gather.2.cloned.1.call-start = ((), (), s32[]{:S(2)}) async-start(), calls=%async_computation.2 | async-start | bytes 1081344 | tf_op jit(solution)/shard_map/all_gather | solution.py:60
  445.9 7.0 %copy-start.4 = (f32[1024,64]{0,1:T(8,128)}, f32[1024,64]{0,1:T(8,128)S(1)}, u32[]{:S(2)}) copy-start(f32[1024,64]{0,1:T(8,128)S(1)} %broadcast_multiply_fusion) | copy-start | bytes 786436
  447.8 1.3 copy-start.3
Sparse Core Ops, SparseCore 0:
  12.1 143.6 all-reduce.2
  195.8 249.0 all-reduce.4
  450.0 74.8 all-gather.1
where the time goes:
time: 534 us
  waiting for transfers between devices  465 us (87%)
  blocking collectives  20.7 us (4%)
  other arithmetic  17.4 us (3%)
  between operations  14.5 us (3%)
  matrix products  11.4 us (2%)
    psum x1, waiting for transfers between devices, on_device(): right_factor = lax.psum(projected, ('rep', 'shard')) / replicas  249 us
    psum x1, waiting for transfers between devices, on_device(): factor = lax.psum(local_factor, 'rep') / replicas  144 us
    all_gather x1, waiting for transfers between devices, on_device(): lax.all_gather(master_out.astype(jnp.bfloat16), 'rep', axis=0, tiled=True)  72 us
    psum x1, blocking collectives, on_device(): gram = lax.psum(gram_part, 'shard')  20.7 us
  transfers between devices with their start and end apart: 3, of which 3 were waited for; matrix products, arithmetic and copies ran while one was open for 1% of the time, Pallas kernels for 0%

commit v1 on v0

--- a/solution.py
+++ b/solution.py
@@ -40,7 +40,7 @@
     inverse = lower_inverse(gram)
     unit_basis = times_inverse(factor, inverse)
     projected = jnp.dot(merged, unit_basis, precision=HIGHEST, preferred_element_type=jnp.float32)
-    right_factor = lax.psum(projected, ("rep", "shard")) / replicas
+    right_factor = lax.psum(lax.psum(projected, "shard"), "rep") / replicas
     approx = lax.dot_general(
         right_factor,
         unit_basis,

time: 534 us -> 494 us (0.925)
  waiting for transfers between devices: 465 us -> 425 us
    psum x1 -> x2, waiting for transfers between devices: 249 us -> 211 us  [on_device(): right_factor = lax.psum(lax.psum(projected, 'shard'), 'rep') / replicas]
  transfers between devices with their start and end apart: 3 -> 4, of which waited for: 3 -> 4; matrix products, arithmetic and copies ran while one was open for 1% -> 1% of each run, Pallas kernels for 0% -> 0%
where the time goes in v1:
time: 494 us; the launch traced here: 493 us
  waiting for transfers between devices  425 us (86%)
  blocking collectives  20.7 us (4%)
  other arithmetic  17.4 us (4%)
  between operations  14.5 us (3%)
  matrix products  11.4 us (2%)
    psum x2, waiting for transfers between devices, on_device(): right_factor = lax.psum(lax.psum(projected, 'shard'), 'rep') / replicas  211 us
    psum x1, waiting for transfers between devices, on_device(): factor = lax.psum(local_factor, 'rep') / replicas  144 us
    all_gather x1, waiting for transfers between devices, on_device(): lax.all_gather(master_out.astype(jnp.bfloat16), 'rep', axis=0, tiled=True)  70.3 us
    psum x1, blocking collectives, on_device(): gram = lax.psum(gram_part, 'shard')  20.7 us
  transfers between devices with their start and end apart: 4, of which 4 were waited for; matrix products, arithmetic and copies ran while one was open for 1% of the time, Pallas kernels for 0%

profile of v1, /device:TPU:2, one launch (start us, length us, event | category | flops | bytes accessed | tf_op | source)
XLA Modules:
  0.0 493.3 jit_solution(8741388548655898110)
XLA Ops:
  7.2 0.0 copy-start
  7.2 0.0 copy-start.1
  7.2 0.0 copy-start.2
  7.2 0.0 all-reduce.4.cloned.1.call-start
  7.2 0.9 copy-done
  8.1 3.8 fusion.2
  12.0 0.0 all-reduce.4.cloned.1.call-update
  12.0 0.0 all-reduce.6.cloned.1.call-start
  12.0 143.7 %all-reduce.4.cloned.1.call-done = f32[512,64]{0,1:T(8,128)} async-done(((f32[512,64]{0,1:T(8,128)}), f32[512,64]{0,1:T(8,128)}) %all-reduce.4.cloned.1.call-update) | async-done | bytes 131088 | tf_op jit(solution)/shard_map/psum | solution.py:37
  155.8 1.2 fusion.8
  157.0 20.7 %psum.29 = f32[64,64]{1,0:T(8,128)S(1)} all-reduce(f32[64,64]{1,0:T(8,128)S(1)} %fusion.8), channel_id=1, replica_groups=mesh['rep'=32,'shard'=8] {'shard'}, use_global_device_ids=true, to_apply=%region_1.0 | all-reduce | flops 4096 | bytes 32768 | tf_op jit(solution)/shard_map/psum | solution.py:39
  177.7 0.6 select_reduce_fusion.1
  179.0 0.1 copy.12
  179.1 5.8 %cholesky.18 = f32[64,64]{1,0:T(8,128)S(1)} custom-call(f32[64,64]{1,0:T(8,128)S(1)} %fusion.16), custom_call_target="Cholesky" | custom-call | tf_op jit(solution)/shard_map/jit(cholesky)/cholesky | solution.py:19
  185.0 0.6 compare_reduce_fusion
  185.6 0.7 fusion.13
  186.3 4.9 custom-call.7
  191.2 0.2 fusion.14
  191.4 1.2 fusion.6
  192.6 0.0 copy-done.1
  192.6 0.0 copy-done.2
  192.6 3.0 fusion
  195.6 0.0 copy-start.5
  195.6 0.0 copy-start.6
  195.6 0.0 copy-start.7
  195.6 0.0 all-reduce.6.cloned.1.call-update
  195.7 0.0 all-reduce.8.cloned.1.call-start
  195.7 61.6 %all-reduce.6.cloned.1.call-done = f32[1024,64]{0,1:T(8,128)} async-done(((f32[1024,64]{0,1:T(8,128)}), f32[1024,64]{0,1:T(8,128)}) %all-reduce.6.cloned.1.call-update) | async-done | bytes 262160 | tf_op jit(solution)/shard_map/psum | solution.py:43
  257.3 0.0 all-reduce.8.cloned.1.call-update
  257.3 0.0 all-gather.2.cloned.1.call-start
  257.4 148.9 %all-reduce.8.cloned.1.call-done = f32[1024,64]{0,1:T(8,128)} async-done(((f32[1024,64]{0,1:T(8,128)}), f32[1024,64]{0,1:T(8,128)}) %all-reduce.8.cloned.1.call-update) | async-done | bytes 262160 | tf_op jit(solution)/shard_map/psum | solution.py:43
  406.3 1.0 broadcast_multiply_fusion
  407.3 0.0 copy-start.4
  407.3 1.8 fusion.21
  409.2 0.0 copy-start.3
  409.2 1.3 copy-done.3
  410.5 0.0 copy-done.5
  410.5 0.0 copy-done.6
  410.5 0.0 copy-done.7
  410.5 0.7 fusion.19
  411.2 0.0 all-gather.2.cloned.1.call-update
  411.2 3.0 fusion.5
  414.3 0.0 copy-done.4
  414.3 70.3 %all-gather.2.cloned.1.call-done = bf16[1024,512]{1,0:T(8,128)(2,1)} async-done(((bf16[32,512]{1,0:T(8,128)(2,1)}), bf16[1024,512]{1,0:T(8,128)(2,1)}) %all-gather.2.cloned.1.call-update) | async-done | bytes 1048592 | tf_op jit(solution)/shard_map/all_gather | solution.py:60
  484.5 2.3 copy.17
  (3 shorter events, 0.1 us)
Async XLA Ops:
  7.2 1.0 copy-start
  7.2 185.4 %copy-start.1 = (bf16[1,1024,512]{2,1,0:T(8,128)(2,1)S(1)}, bf16[1,1024,512]{2,1,0:T(8,128)(2,1)}, u32[]{:S(2)}) copy-start(bf16[1,1024,512]{2,1,0:T(8,128)(2,1)} %param.7) | copy-start | bytes 3145732
  7.2 185.4 %copy-start.2 = (bf16[1,1024,512]{2,1,0:T(8,128)(2,1)S(1)}, bf16[1,1024,512]{2,1,0:T(8,128)(2,1)}, u32[]{:S(2)}) copy-start(bf16[1,1024,512]{2,1,0:T(8,128)(2,1)} %param.6) | copy-start | bytes 3145732
  7.2 148.6 %all-reduce.4.cloned.1.call-start = ((), (), s32[]{:S(2)}) async-start(), calls=%async_computation | async-start | bytes 262144 | tf_op jit(solution)/shard_map/psum | solution.py:37
  12.0 245.3 %all-reduce.6.cloned.1.call-start = ((), (), s32[]{:S(2)}) async-start(), calls=%async_computation.1 | async-start | bytes 524288 | tf_op jit(solution)/shard_map/psum | solution.py:43
  195.6 214.9 %copy-start.5 = (f32[32,512]{1,0:T(8,128)S(1)}, f32[32,512]{1,0:T(8,128)}, u32[]{:S(2)}) copy-start(f32[32,512]{1,0:T(8,128)} %param.9) | copy-start | bytes 196612
  195.6 214.9 %copy-start.6 = (f32[32,512]{1,0:T(8,128)S(1)}, f32[32,512]{1,0:T(8,128)}, u32[]{:S(2)}) copy-start(f32[32,512]{1,0:T(8,128)} %param.11) | copy-start | bytes 196612
  195.6 214.9 %copy-start.7 = (f32[32,512]{1,0:T(8,128)S(1)}, f32[32,512]{1,0:T(8,128)}, u32[]{:S(2)}) copy-start(f32[32,512]{1,0:T(8,128)} %param.10) | copy-start | bytes 196612
  195.7 210.6 %all-reduce.8.cloned.1.call-start = ((), (), s32[]{:S(2)}) async-start(), calls=%async_computation.2 | async-start | bytes 524288 | tf_op jit(solution)/shard_map/psum | solution.py:43
  257.3 227.2 %all-gather.2.cloned.1.call-start = ((), (), s32[]{:S(2)}) async-start(), calls=%async_computation.3 | async-start | bytes 1081344 | tf_op jit(solution)/shard_map/all_gather | solution.py:60
  407.3 7.0 %copy-start.4 = (f32[1024,64]{0,1:T(8,128)}, f32[1024,64]{0,1:T(8,128)S(1)}, u32[]{:S(2)}) copy-start(f32[1024,64]{0,1:T(8,128)S(1)} %broadcast_multiply_fusion) | copy-start | bytes 786436
  409.2 1.3 copy-start.3
Sparse Core Ops, SparseCore 0:
  12.1 143.6 all-reduce.3
  195.8 61.4 all-reduce.5
  260.8 145.4 all-reduce.7
  411.4 73.1 all-gather.1
